TPU v7x, 32 devices: a whole 2x2x4 slice. The times are simulated.
32 devices in a mesh: mp: 2 (over x), width: 2 (over y), hidden: 8 (over z, core).
Axes of the slice: x: 2, y: 2, z: 4, core: 2. Of those that a mesh axis runs over, the one named last changes fastest.
Arguments:
- residual_in: bfloat16 [2, 512, 3584], P('mp', 'hidden'), may hold values from -6 to 6
- gate_weight: bfloat16 [2, 14336, 3584], P('mp', ('width', 'hidden')), may hold values from -0.09375 to 0.09375
- up_weight: bfloat16 [2, 14336, 3584], P('mp', ('width', 'hidden')), may hold values from -0.09375 to 0.09375
- down_weight: bfloat16 [2, 14336, 3584], P('mp', ('width', 'hidden')), may hold values from -0.046875 to 0.046875
- enc_weight: float32 [7168, 16384], P(('mp', 'width'), 'hidden'), may hold values from -0.0625 to 0.0625
- enc_bias: float32 [16384], P('hidden'), may hold values from -3 to 3
- dec_weight: float32 [16384, 7168], P('hidden', ('mp', 'width')), may hold values from -0.25 to 0.25
- dec_bias: float32 [7168], P(('mp', 'width')), may hold values from -2 to 2
Outputs:
- mlp_acts: bfloat16 [2, 512, 3584], P('mp', 'hidden', 'width')
- latents: float32 [512, 16384], P(None, 'hidden')
- grad_enc: float32 [7168, 16384], P(('mp', 'width'), 'hidden')
- grad_dec: float32 [16384, 7168], P('hidden', ('mp', 'width'))
- grad_enc_bias: float32 [16384], P('hidden')
- grad_dec_bias: float32 [7168], P(('mp', 'width'))
All inputs are finite; a program needn't handle non-finite values.
Results may differ from a plain program's by a relative error of at most 0.0058.
Values may be sent and summed in bfloat16 or wider, within the bound.
A program may use at most 192 MiB of HBM per device.

v0:
```python
import jax
import jax.numpy as jnp
from jax import lax
from jax.sharding import PartitionSpec as P

TOKENS = 512
sharpness = 8.0
sparsity_coef = 0.02
norm_floor = 1e-06
highest = lax.Precision.HIGHEST


def body(
    residual_in, gate_weight, up_weight, down_weight, enc_weight, enc_bias, dec_weight, dec_bias
):
    last_last = (((1,), (1,)), ((), ()))
    first_first = (((0,), (0,)), ((), ()))
    gathered = lax.all_gather(residual_in[0], "hidden", axis=0, tiled=True)
    gate_act = lax.dot_general(
        gathered, gate_weight[0], last_last, preferred_element_type=jnp.float32
    )
    up_act = lax.dot_general(gathered, up_weight[0], last_last, preferred_element_type=jnp.float32)
    hidden_act = (jax.nn.gelu(gate_act, approximate=True) * up_act).astype(jnp.bfloat16)
    down_local = down_weight[0]
    row_sums = lax.psum_scatter(
        jnp.dot(hidden_act, down_local, preferred_element_type=jnp.float32),
        "hidden",
        scatter_dimension=0,
        tiled=True,
    )
    model_sums = lax.psum_scatter(row_sums, "width", scatter_dimension=1, tiled=True)
    mlp_acts = model_sums.astype(jnp.bfloat16)
    coder_in = lax.all_gather(mlp_acts, "hidden", axis=0, tiled=True).astype(jnp.float32)
    enc_partial = jnp.dot(coder_in, enc_weight, precision=highest)
    model_index = lax.axis_index("mp")
    squares = jnp.sum(dec_weight * dec_weight, axis=1)
    square_pair = jnp.where(jnp.arange(2)[:, None] == model_index, squares[None, :], 0.0)
    pre_sum, square_sums = lax.psum((enc_partial, square_pair), ("mp", "width"))
    pre_act = pre_sum + enc_bias
    latents = jax.nn.softplus(sharpness * pre_act) / sharpness
    dec_norms = jnp.sqrt(square_sums + norm_floor)
    recon_part = jnp.dot(latents, dec_weight, precision=highest)
    own_rebuilt = lax.psum_scatter(recon_part, "hidden", scatter_dimension=0, tiled=True) + dec_bias
    own_grad = 2.0 / TOKENS * (own_rebuilt - mlp_acts.astype(jnp.float32))
    err_grad = lax.all_gather(own_grad.astype(jnp.bfloat16), "hidden", axis=0, tiled=True).astype(
        own_grad.dtype
    )
    grad_dec_bias = jnp.sum(err_grad, axis=0)
    back_part = lax.dot_general(
        err_grad, dec_weight, last_last, precision=highest, preferred_element_type=jnp.float32
    )
    lat_grad = lax.psum(back_part.astype(jnp.bfloat16), ("mp", "width")).astype(
        jnp.float32
    ) + sparsity_coef * (dec_norms[0] + dec_norms[1])
    pre_grad = lat_grad * jax.nn.sigmoid(sharpness * pre_act)
    grad_enc_bias = jnp.sum(pre_grad, axis=0)
    grad_enc = lax.dot_general(
        coder_in, pre_grad, first_first, precision=highest, preferred_element_type=jnp.float32
    )
    latent_totals = jnp.sum(latents, axis=0)
    own_norm = jnp.where(model_index == 0, dec_norms[0], dec_norms[1])
    grad_dec = lax.dot_general(
        latents, err_grad, first_first, precision=highest, preferred_element_type=jnp.float32
    )
    grad_dec = grad_dec + sparsity_coef * (latent_totals / own_norm)[:, None] * dec_weight
    return (mlp_acts[None], latents, grad_enc, grad_dec, grad_enc_bias, grad_dec_bias)


def solution(mesh):
    return jax.shard_map(
        body,
        mesh=mesh,
        in_specs=(
            P("mp", "hidden", None),
            P("mp", ("width", "hidden"), None),
            P("mp", ("width", "hidden"), None),
            P("mp", ("width", "hidden"), None),
            P(("mp", "width"), "hidden"),
            P("hidden"),
            P("hidden", ("mp", "width")),
            P(("mp", "width")),
        ),
        out_specs=(
            P("mp", "hidden", "width"),
            P(None, "hidden"),
            P(("mp", "width"), "hidden"),
            P("hidden", ("mp", "width")),
            P("hidden"),
            P(("mp", "width")),
        ),
        check_vma=False,
    )
```

profile of v0, /device:TPU:0, one launch (start us, length us, event | category | flops | bytes accessed | tf_op | source)
XLA Modules:
  0.0 549.1 jit_solution(14673929088239518730)
XLA Ops:
  7.9 47.0 %all-gather.9.cloned.1.call-done = bf16[1,512,3584]{2,1,0:T(8,128)(2,1)} async-done(((bf16[1,64,3584]{2,1,0:T(8,128)(2,1)}), bf16[1,512,3584]{2,1,0:T(8,128)(2,1)}) %all-gather.9.cloned.1.call-update) | async-done | bytes 3670032 | tf_op jit(solution)/shard_map/all_gather | solution.py:18
  54.9 9.6 %fusion.4 = f32[512,896]{1,0:T(8,128)S(1)} fusion(bf16[1,896,3584]{2,1,0:T(8,128)(2,1)} %param.9, bf16[1,512,3584]{2,1,0:T(8,128)(2,1)} %all-gather.9.cloned.1.call-done), kind=kOutput, calls=%fused_computation.7 | convolution fusion | flops 3288334336 | bytes 11927552 | tf_op jit(solution)/shard_map/dot_general | solution.py:19
  64.6 7.1 %fusion.17 = bf16[512,896]{1,0:T(8,128)(2,1)S(1)} fusion(f32[512,896]{1,0:T(8,128)S(1)} %fusion.4, bf16[1,896,3584]{2,1,0:T(8,128)(2,1)} %param.10, bf16[1,512,3584]{2,1,0:T(8,128)(2,1)S(1)} %copy-done.7), kind=kOutput, calls=%fused_computation.25 | convolution fusion | flops 3292921856 | bytes 12845056 | tf_op jit(solution)/shard_map/dot_general | solution.py:22
  71.7 6.0 %fusion = f32[512,3584]{1,0:T(8,128)} fusion(bf16[512,896]{1,0:T(8,128)(2,1)S(1)} %fusion.17, bf16[1,896,3584]{2,1,0:T(8,128)(2,1)S(1)} %bitcast.36), kind=kOutput, calls=%fused_computation.3 | convolution fusion | flops 3288334336 | bytes 14680064 | tf_op jit(solution)/shard_map/dot_general | solution.py:26
  77.9 78.6 %reduce-scatter.4.cloned.1.call-done = f32[64,3584]{1,0:T(8,128)} async-done(((f32[512,3584]{1,0:T(8,128)}), f32[64,3584]{1,0:T(8,128)}) %reduce-scatter.4.cloned.1.call-update) | async-done | bytes 917520 | tf_op jit(solution)/shard_map/reduce_scatter | solution.py:25
  156.5 19.6 %reduce-scatter.6.cloned.1.call-done = f32[64,1792]{1,0:T(8,128)} async-done(((f32[64,3584]{1,0:T(8,128)}), f32[64,1792]{1,0:T(8,128)}) %reduce-scatter.6.cloned.1.call-update) | async-done | bytes 458768 | tf_op jit(solution)/shard_map/reduce_scatter | solution.py:31
  176.1 1.7 convert_element_type.23
  178.2 27.0 %all-gather.5.cloned.1.call-done = bf16[512,1792]{1,0:T(8,128)(2,1)} async-done(((bf16[64,1792]{1,0:T(8,128)(2,1)}), bf16[512,1792]{1,0:T(8,128)(2,1)}) %all-gather.5.cloned.1.call-update) | async-done | bytes 1835024 | tf_op jit(solution)/shard_map/all_gather | solution.py:33
  205.2 16.9 %fusion.26 = f32[512,2048]{1,0:T(8,128)} fusion(bf16[512,1792]{1,0:T(8,128)(2,1)} %all-gather.5.cloned.1.call-done, f32[1792,2048]{1,0:T(8,128)} %param.12), kind=kOutput, calls=%fused_computation.36 | convolution fusion | flops 22548578304 | bytes 20709376 | tf_op jit(solution)/shard_map/dot_general | solution.py:34
  222.5 102.8 %all-reduce.3.cloned.1.call-done = f32[512,2048]{1,0:T(8,128)} async-done(((f32[512,2048]{1,0:T(8,128)}), f32[512,2048]{1,0:T(8,128)}) %all-reduce.3.cloned.1.call-update) | async-done | bytes 4194320 | tf_op jit(solution)/shard_map/psum | solution.py:38
  325.3 4.9 fusion.24
  330.2 2.0 copy-done
  332.2 26.6 %fusion.27 = f32[512,1792]{1,0:T(8,128)} fusion(f32[512,2048]{1,0:T(8,128)S(1)} %get-tuple-element.7, f32[2048,1792]{1,0:T(8,128)} %param.14), kind=kOutput, calls=%fused_computation.37 | convolution fusion | flops 22548578304 | bytes 22544384 | tf_op jit(solution)/shard_map/dot_general | solution.py:42
  359.0 45.1 %reduce-scatter.8.cloned.1.call-done = f32[64,1792]{1,0:T(8,128)} async-done(((f32[512,1792]{1,0:T(8,128)}), f32[64,1792]{1,0:T(8,128)}) %reduce-scatter.8.cloned.1.call-update) | async-done | bytes 458768 | tf_op jit(solution)/shard_map/reduce_scatter | solution.py:43
  404.1 1.8 multiply_convert_fusion
  405.9 6.2 %multiply_reduce_fusion = f32[2048]{0:T(1024)S(1)} fusion(f32[2048,1792]{1,0:T(8,128)} %param.14), kind=kLoop, calls=%fused_computation.1 | loop fusion | flops 7337984 | bytes 14688256 | tf_op jit(solution)/shard_map/reduce_sum | solution.py:36
  412.2 16.5 %psum.23 = f32[2,2048]{1,0:T(2,128)S(1)} all-reduce(f32[2,2048]{1,0:T(2,128)S(1)} %broadcast_select_fusion), channel_id=1, replica_groups=mesh['mp'=2,'width'=2,'hidden'=8] {'mp','width'}, use_global_device_ids=true, to_apply=%region_6.7 | all-reduce | flops 4096 | bytes 32768 | tf_op jit(solution)/shard_map/psum | solution.py:38
  428.8 2.9 all-gather.7.cloned.1.call-done
  431.7 18.4 %convolution_convert_fusion = bf16[512,2048]{1,0:T(8,128)(2,1)} fusion(bf16[512,1792]{1,0:T(8,128)(2,1)} %all-gather.7.cloned.1.call-done, f32[2048,1792]{1,0:T(8,128)} %param.14), kind=kOutput, calls=%fused_computation.15 | convolution fusion | flops 22549626880 | bytes 18612224 | tf_op jit(solution)/shard_map/dot_general | solution.py:49
  450.8 0.9 convert_reduce_fusion
  451.7 19.6 %multiply_add_fusion = f32[2048,1792]{1,0:T(8,128)} fusion(f32[2048,1792]{1,0:T(8,128)} %param.14, f32[512,2048]{1,0:T(8,128)} %copy-done, bf16[512,1792]{1,0:T(8,128)(2,1)S(1)} %copy-done.2, f32[2048]{0:T(1024)S(1)} %divide_multiply_fusion.1), kind=kOutput, calls=%fused_computation | convolution fusion | flops 22555918336 | bytes 35397632 | tf_op jit(solution)/shard_map/dot_general | solution.py:62
  471.3 47.8 %all-reduce.5.cloned.1.call-done = bf16[512,2048]{1,0:T(8,128)(2,1)} async-done(((bf16[512,2048]{1,0:T(8,128)(2,1)}), bf16[512,2048]{1,0:T(8,128)(2,1)}) %all-reduce.5.cloned.1.call-update) | async-done | bytes 2097168 | tf_op jit(solution)/shard_map/psum | solution.py:52
  519.2 5.0 fusion.22
  524.1 17.9 %fusion.23 = f32[1792,2048]{1,0:T(8,128)} fusion(bf16[512,1792]{1,0:T(8,128)(2,1)} %all-gather.5.cloned.1.call-done, bf16[512,2048]{1,0:T(8,128)(2,1)S(1)} %copy-done.4, f32[512,2048]{1,0:T(8,128)S(1)} %copy-done.1, f32[2048]{0:T(1024)S(1)} %bitcast.33, f32[2048]{0:T(1024)S(1)} %copy-done.5), kind=kOutput, calls=%fused_computation.34 | convolution fusion | flops 22556966912 | bytes 22822912 | tf_op jit(solution)/shard_map/dot_general | solution.py:57
  (42 shorter events, 2.6 us)
Async XLA Ops:
  7.2 47.7 %all-gather.9.cloned.1.call-start = ((), (), s32[]{:S(2)}) async-start(), calls=%async_computation.10 | async-start | bytes 4128768 | tf_op jit(solution)/shard_map/all_gather | solution.py:18
  7.9 148.5 %reduce-scatter.4.cloned.1.call-start = ((), (), s32[]{:S(2)}) async-start(), calls=%async_computation.3 | async-start | bytes 8257536 | tf_op jit(solution)/shard_map/reduce_scatter | solution.py:25
  54.9 9.6 %copy-start.7 = (bf16[1,512,3584]{2,1,0:T(8,128)(2,1)S(1)}, bf16[1,512,3584]{2,1,0:T(8,128)(2,1)}, u32[]{:S(2)}) copy-start(bf16[1,512,3584]{2,1,0:T(8,128)(2,1)} %all-gather.9.cloned.1.call-done) | copy-start | bytes 11010052
  54.9 16.8 %slice-start = ((s8[6422528]{0:T(1024)(128)(4,1)}), s8[4194304]{0:T(1024)(128)(4,1)S(1)}, s32[]{:S(2)}) async-start(s8[6422528]{0:T(1024)(128)(4,1)} %bitcast.35), calls=%async_computation.11 | async-start | bytes 8388608
  64.6 7.2 %slice-start.1 = ((s8[6422528]{0:T(1024)(128)(4,1)}), s8[2228224]{0:T(1024)(128)(4,1)S(1)}, s32[]{:S(2)}) async-start(s8[6422528]{0:T(1024)(128)(4,1)} %bitcast.35), calls=%async_computation.12 | async-start | bytes 4456448
  77.8 98.3 %reduce-scatter.6.cloned.1.call-start = ((), (), s32[]{:S(2)}) async-start(), calls=%async_computation.4 | async-start | bytes 1376256 | tf_op jit(solution)/shard_map/reduce_scatter | solution.py:31
  156.4 48.8 %all-gather.5.cloned.1.call-start = ((), (), s32[]{:S(2)}) async-start(), calls=%async_computation.5 | async-start | bytes 2064384 | tf_op jit(solution)/shard_map/all_gather | solution.py:33
  177.9 147.4 %all-reduce.3.cloned.1.call-start = ((), (), s32[]{:S(2)}) async-start(), calls=%async_computation.6 | async-start | bytes 8388608 | tf_op jit(solution)/shard_map/psum | solution.py:38
  222.1 103.2 %copy-start.5 = (f32[2048]{0:T(1024)S(1)}, f32[2048]{0:T(1024)}, u32[]{:S(2)}) copy-start(f32[2048]{0:T(1024)} %param.13) | copy-start | bytes 24580
  222.1 181.9 %reduce-scatter.8.cloned.1.call-start = ((), (), s32[]{:S(2)}) async-start(), calls=%async_computation.7 | async-start | bytes 4128768 | tf_op jit(solution)/shard_map/reduce_scatter | solution.py:43
  330.2 2.0 copy-start
  332.2 71.8 %copy-start.3 = (f32[64,1792]{1,0:T(8,128)S(1)}, f32[64,1792]{1,0:T(8,128)}, u32[]{:S(2)}) copy-start(f32[64,1792]{1,0:T(8,128)} %reduce-scatter.6.cloned.1.call-done) | copy-start | bytes 1376260
  332.2 71.8 %copy-start.6 = (f32[1792]{0:T(1024)S(1)}, f32[1792]{0:T(1024)}, u32[]{:S(2)}) copy-start(f32[1792]{0:T(1024)} %param.15) | copy-start | bytes 21508
  358.9 72.7 %all-gather.7.cloned.1.call-start = ((), (), s32[]{:S(2)}) async-start(), calls=%async_computation.8 | async-start | bytes 2064384 | tf_op jit(solution)/shard_map/all_gather | solution.py:45
  405.8 113.3 %all-reduce.5.cloned.1.call-start = ((), (), s32[]{:S(2)}) async-start(), calls=%async_computation.9 | async-start | bytes 4194304 | tf_op jit(solution)/shard_map/psum | solution.py:52
  431.7 19.2 %copy-start.2 = (bf16[512,1792]{1,0:T(8,128)(2,1)S(1)}, bf16[512,1792]{1,0:T(8,128)(2,1)}, u32[]{:S(2)}) copy-start(bf16[512,1792]{1,0:T(8,128)(2,1)} %all-gather.7.cloned.1.call-done) | copy-start | bytes 5505028
  519.1 5.0 copy-start.1
  519.1 5.0 copy-start.4
Sparse Core Ops, SparseCore 0:
  9.6 45.2 all-gather.8
  77.9 78.4 reduce-scatter.3
  158.7 17.3 reduce-scatter.5
  178.2 26.9 all-gather.4
  222.2 103.0 all-reduce.2
  359.0 44.9 reduce-scatter.7
  406.3 25.3 all-gather.6
  450.2 68.8 all-reduce.4
where the time goes:
time: 555 us; the launch traced here: 549 us
  waiting for transfers between devices  372 us (67%)
  matrix products  122 us (22%)
  other arithmetic  21.3 us (4%)
  blocking collectives  16.5 us (3%)
  between operations  14.5 us (3%)
    psum x1, waiting for transfers between devices, body(): pre_sum, square_sums = lax.psum((enc_partial, square_pair), ('mp', 'width'))  103 us
    reduce_scatter x1, waiting for transfers between devices, body(): lax.psum_scatter(jnp.dot(hidden_act, down_local, preferred_element_type=j...  78.6 us
    psum x1, waiting for transfers between devices, body(): lax.psum(back_part.astype(jnp.bfloat16), ('mp', 'width'))  47.8 us
    all_gather x1, waiting for transfers between devices, body(): gathered = lax.all_gather(residual_in[0], 'hidden', axis=0, tiled=True)  47 us
    reduce_scatter x1, waiting for transfers between devices, body(): lax.psum_scatter(recon_part, 'hidden', scatter_dimension=0, tiled=True)  45.1 us
    all_gather x1, waiting for transfers between devices, body(): lax.all_gather(mlp_acts, 'hidden', axis=0, tiled=True).astype(jnp.float32)  27 us
    dot_general x1, matrix products, body(): recon_part = jnp.dot(latents, dec_weight, precision=highest)  26.6 us
    reduce_scatter x1, waiting for transfers between devices, body(): lax.psum_scatter(row_sums, 'width', scatter_dimension=1, tiled=True)  19.6 us
  transfers between devices with their start and end apart: 8, of which 8 were waited for; matrix products, arithmetic and copies ran while one was open for 5% of the time, Pallas kernels for 0%

commit v1 on v0

--- a/solution.py
+++ b/solution.py
@@ -49,7 +49,7 @@
     back_part = lax.dot_general(
         err_grad, dec_weight, last_last, precision=highest, preferred_element_type=jnp.float32
     )
-    lat_grad = lax.psum(back_part.astype(jnp.bfloat16), ("mp", "width")).astype(
+    lat_grad = lax.psum(lax.psum(back_part.astype(jnp.bfloat16), "width"), "mp").astype(
         jnp.float32
     ) + sparsity_coef * (dec_norms[0] + dec_norms[1])
     pre_grad = lat_grad * jax.nn.sigmoid(sharpness * pre_act)

time: 555 us -> 612 us (1.10)
  waiting for transfers between devices: 372 us -> 431 us
    psum x1 -> x2, waiting for transfers between devices: 47.8 us -> 84.7 us  [the longest x1 44.8 us: body(): lax.psum(lax.psum(back_part.astype(jnp.bfloat16), 'width'), 'mp')]
    all_gather x1, waiting for transfers between devices: 2.86 us -> 25.2 us  [body(): lax.all_gather(own_grad.astype(jnp.bfloat16), 'hidden', axis=0, tiled=True)]
  transfers between devices with their start and end apart: 8 -> 9, of which waited for: 8 -> 9; matrix products, arithmetic and copies ran while one was open for 5% -> 4% of each run, Pallas kernels for 0% -> 0%
where the time goes in v1:
time: 612 us; the launch traced here: 606 us
  waiting for transfers between devices  431 us (70%)
  matrix products  120 us (20%)
  other arithmetic  21.6 us (4%)
  blocking collectives  16.4 us (3%)
  between operations  14.2 us (2%)
    psum x1, waiting for transfers between devices, body(): pre_sum, square_sums = lax.psum((enc_partial, square_pair), ('mp', 'width'))  103 us
    reduce_scatter x1, waiting for transfers between devices, body(): lax.psum_scatter(jnp.dot(hidden_act, down_local, preferred_element_type=j...  78.6 us
    all_gather x1, waiting for transfers between devices, body(): gathered = lax.all_gather(residual_in[0], 'hidden', axis=0, tiled=True)  47 us
    reduce_scatter x1, waiting for transfers between devices, body(): lax.psum_scatter(recon_part, 'hidden', scatter_dimension=0, tiled=True)  45.1 us
    psum x1, waiting for transfers between devices, body(): lax.psum(lax.psum(back_part.astype(jnp.bfloat16), 'width'), 'mp')  44.8 us
    psum x1, waiting for transfers between devices, body(): lax.psum(back_part.astype(jnp.bfloat16), 'width')  40 us
    all_gather x1, waiting for transfers between devices, body(): lax.all_gather(mlp_acts, 'hidden', axis=0, tiled=True).astype(jnp.float32)  27 us
    dot_general x1, matrix products, body(): recon_part = jnp.dot(latents, dec_weight, precision=highest)  26.6 us
  transfers between devices with their start and end apart: 9, of which 9 were waited for; matrix products, arithmetic and copies ran while one was open for 4% of the time, Pallas kernels for 0%

profile of v1, /device:TPU:0, one launch (start us, length us, event | category | flops | bytes accessed | tf_op | source)
XLA Modules:
  0.0 606.2 jit_solution(2779686343507140764)
XLA Ops:
  7.9 47.0 %all-gather.9.cloned.1.call-done = bf16[1,512,3584]{2,1,0:T(8,128)(2,1)} async-done(((bf16[1,64,3584]{2,1,0:T(8,128)(2,1)}), bf16[1,512,3584]{2,1,0:T(8,128)(2,1)}) %all-gather.9.cloned.1.call-update) | async-done | bytes 3670032 | tf_op jit(solution)/shard_map/all_gather | solution.py:18
  54.9 9.6 %fusion.4 = f32[512,896]{1,0:T(8,128)S(1)} fusion(bf16[1,896,3584]{2,1,0:T(8,128)(2,1)} %param.9, bf16[1,512,3584]{2,1,0:T(8,128)(2,1)} %all-gather.9.cloned.1.call-done), kind=kOutput, calls=%fused_computation.7 | convolution fusion | flops 3288334336 | bytes 11927552 | tf_op jit(solution)/shard_map/dot_general | solution.py:19
  64.6 7.1 %fusion.17 = bf16[512,896]{1,0:T(8,128)(2,1)S(1)} fusion(f32[512,896]{1,0:T(8,128)S(1)} %fusion.4, bf16[1,896,3584]{2,1,0:T(8,128)(2,1)} %param.10, bf16[1,512,3584]{2,1,0:T(8,128)(2,1)S(1)} %copy-done.7), kind=kOutput, calls=%fused_computation.25 | convolution fusion | flops 3292921856 | bytes 12845056 | tf_op jit(solution)/shard_map/dot_general | solution.py:22
  71.7 6.0 fusion
  77.9 78.6 %reduce-scatter.4.cloned.1.call-done = f32[64,3584]{1,0:T(8,128)} async-done(((f32[512,3584]{1,0:T(8,128)}), f32[64,3584]{1,0:T(8,128)}) %reduce-scatter.4.cloned.1.call-update) | async-done | bytes 917520 | tf_op jit(solution)/shard_map/reduce_scatter | solution.py:25
  156.5 19.6 %reduce-scatter.6.cloned.1.call-done = f32[64,1792]{1,0:T(8,128)} async-done(((f32[64,3584]{1,0:T(8,128)}), f32[64,1792]{1,0:T(8,128)}) %reduce-scatter.6.cloned.1.call-update) | async-done | bytes 458768 | tf_op jit(solution)/shard_map/reduce_scatter | solution.py:31
  176.1 1.7 convert_element_type.23
  178.2 27.0 %all-gather.5.cloned.1.call-done = bf16[512,1792]{1,0:T(8,128)(2,1)} async-done(((bf16[64,1792]{1,0:T(8,128)(2,1)}), bf16[512,1792]{1,0:T(8,128)(2,1)}) %all-gather.5.cloned.1.call-update) | async-done | bytes 1835024 | tf_op jit(solution)/shard_map/all_gather | solution.py:33
  205.2 16.9 %fusion.26 = f32[512,2048]{1,0:T(8,128)} fusion(bf16[512,1792]{1,0:T(8,128)(2,1)} %all-gather.5.cloned.1.call-done, f32[1792,2048]{1,0:T(8,128)} %param.12), kind=kOutput, calls=%fused_computation.36 | convolution fusion | flops 22548578304 | bytes 20709376 | tf_op jit(solution)/shard_map/dot_general | solution.py:34
  222.5 102.8 %all-reduce.4.cloned.1.call-done = f32[512,2048]{1,0:T(8,128)} async-done(((f32[512,2048]{1,0:T(8,128)}), f32[512,2048]{1,0:T(8,128)}) %all-reduce.4.cloned.1.call-update) | async-done | bytes 4194320 | tf_op jit(solution)/shard_map/psum | solution.py:38
  325.3 4.9 fusion.24
  330.2 2.0 copy-done
  332.2 26.6 %fusion.27 = f32[512,1792]{1,0:T(8,128)} fusion(f32[512,2048]{1,0:T(8,128)S(1)} %get-tuple-element.7, f32[2048,1792]{1,0:T(8,128)} %param.14), kind=kOutput, calls=%fused_computation.37 | convolution fusion | flops 22548578304 | bytes 22544384 | tf_op jit(solution)/shard_map/dot_general | solution.py:42
  358.9 45.1 %reduce-scatter.8.cloned.1.call-done = f32[64,1792]{1,0:T(8,128)} async-done(((f32[512,1792]{1,0:T(8,128)}), f32[64,1792]{1,0:T(8,128)}) %reduce-scatter.8.cloned.1.call-update) | async-done | bytes 458768 | tf_op jit(solution)/shard_map/reduce_scatter | solution.py:43
  404.0 1.8 multiply_convert_fusion
  406.5 25.2 %all-gather.7.cloned.1.call-done = bf16[512,1792]{1,0:T(8,128)(2,1)} async-done(((bf16[64,1792]{1,0:T(8,128)(2,1)}), bf16[512,1792]{1,0:T(8,128)(2,1)}) %all-gather.7.cloned.1.call-update) | async-done | bytes 1835024 | tf_op jit(solution)/shard_map/all_gather | solution.py:45
  431.6 16.5 %convolution_convert_fusion = bf16[512,2048]{1,0:T(8,128)(2,1)} fusion(bf16[512,1792]{1,0:T(8,128)(2,1)} %all-gather.7.cloned.1.call-done, f32[2048,1792]{1,0:T(8,128)} %param.14), kind=kOutput, calls=%fused_computation.15 | convolution fusion | flops 22549626880 | bytes 18612224 | tf_op jit(solution)/shard_map/dot_general | solution.py:49
  448.3 6.5 %multiply_reduce_fusion = f32[2048]{0:T(1024)S(1)} fusion(f32[2048,1792]{1,0:T(8,128)} %param.14), kind=kLoop, calls=%fused_computation.1 | loop fusion | flops 7337984 | bytes 14688256 | tf_op jit(solution)/shard_map/reduce_sum | solution.py:36
  454.9 16.4 %psum.31 = f32[2,2048]{1,0:T(2,128)S(1)} all-reduce(f32[2,2048]{1,0:T(2,128)S(1)} %broadcast_select_fusion), channel_id=1, replica_groups=mesh['mp'=2,'width'=2,'hidden'=8] {'mp','width'}, use_global_device_ids=true, to_apply=%region_7.8 | all-reduce | flops 4096 | bytes 32768 | tf_op jit(solution)/shard_map/psum | solution.py:38
  471.3 40.0 %all-reduce.6.cloned.1.call-done = bf16[512,2048]{1,0:T(8,128)(2,1)} async-done(((bf16[512,2048]{1,0:T(8,128)(2,1)}), bf16[512,2048]{1,0:T(8,128)(2,1)}) %all-reduce.6.cloned.1.call-update) | async-done | bytes 2097168 | tf_op jit(solution)/shard_map/psum | solution.py:52
  512.9 18.9 %multiply_add_fusion = f32[2048,1792]{1,0:T(8,128)} fusion(f32[2048,1792]{1,0:T(8,128)} %param.14, f32[512,2048]{1,0:T(8,128)} %copy-done, bf16[512,1792]{1,0:T(8,128)(2,1)S(1)} %copy-done.2, f32[2048]{0:T(1024)S(1)} %divide_multiply_fusion.1), kind=kOutput, calls=%fused_computation | convolution fusion | flops 22555918336 | bytes 35397632 | tf_op jit(solution)/shard_map/dot_general | solution.py:62
  531.8 44.8 %all-reduce.8.cloned.1.call-done = bf16[512,2048]{1,0:T(8,128)(2,1)} async-done(((bf16[512,2048]{1,0:T(8,128)(2,1)}), bf16[512,2048]{1,0:T(8,128)(2,1)}) %all-reduce.8.cloned.1.call-update) | async-done | bytes 2097168 | tf_op jit(solution)/shard_map/psum | solution.py:52
  576.6 5.0 fusion.22
  581.6 17.9 %fusion.23 = f32[1792,2048]{1,0:T(8,128)} fusion(bf16[512,1792]{1,0:T(8,128)(2,1)} %all-gather.5.cloned.1.call-done, bf16[512,2048]{1,0:T(8,128)(2,1)S(1)} %copy-done.4, f32[512,2048]{1,0:T(8,128)S(1)} %copy-done.1, f32[2048]{0:T(1024)S(1)} %bitcast.33, f32[2048]{0:T(1024)S(1)} %copy-done.5), kind=kOutput, calls=%fused_computation.34 | convolution fusion | flops 22556966912 | bytes 22822912 | tf_op jit(solution)/shard_map/dot_general | solution.py:57
  (45 shorter events, 4.2 us)
Async XLA Ops:
  7.2 47.7 %all-gather.9.cloned.1.call-start = ((), (), s32[]{:S(2)}) async-start(), calls=%async_computation.11 | async-start | bytes 4128768 | tf_op jit(solution)/shard_map/all_gather | solution.py:18
  7.9 148.5 %reduce-scatter.4.cloned.1.call-start = ((), (), s32[]{:S(2)}) async-start(), calls=%async_computation.3 | async-start | bytes 8257536 | tf_op jit(solution)/shard_map/reduce_scatter | solution.py:25
  54.9 9.6 %copy-start.7 = (bf16[1,512,3584]{2,1,0:T(8,128)(2,1)S(1)}, bf16[1,512,3584]{2,1,0:T(8,128)(2,1)}, u32[]{:S(2)}) copy-start(bf16[1,512,3584]{2,1,0:T(8,128)(2,1)} %all-gather.9.cloned.1.call-done) | copy-start | bytes 11010052
  54.9 16.8 %slice-start = ((s8[6422528]{0:T(1024)(128)(4,1)}), s8[4194304]{0:T(1024)(128)(4,1)S(1)}, s32[]{:S(2)}) async-start(s8[6422528]{0:T(1024)(128)(4,1)} %bitcast.35), calls=%async_computation.12 | async-start | bytes 8388608
  64.6 7.2 %slice-start.1 = ((s8[6422528]{0:T(1024)(128)(4,1)}), s8[2228224]{0:T(1024)(128)(4,1)S(1)}, s32[]{:S(2)}) async-start(s8[6422528]{0:T(1024)(128)(4,1)} %bitcast.35), calls=%async_computation.13 | async-start | bytes 4456448
  77.8 98.3 %reduce-scatter.6.cloned.1.call-start = ((), (), s32[]{:S(2)}) async-start(), calls=%async_computation.4 | async-start | bytes 1376256 | tf_op jit(solution)/shard_map/reduce_scatter | solution.py:31
  156.4 48.7 %all-gather.5.cloned.1.call-start = ((), (), s32[]{:S(2)}) async-start(), calls=%async_computation.5 | async-start | bytes 2064384 | tf_op jit(solution)/shard_map/all_gather | solution.py:33
  177.9 147.4 %all-reduce.4.cloned.1.call-start = ((), (), s32[]{:S(2)}) async-start(), calls=%async_computation.6 | async-start | bytes 8388608 | tf_op jit(solution)/shard_map/psum | solution.py:38
  222.1 103.2 %copy-start.5 = (f32[2048]{0:T(1024)S(1)}, f32[2048]{0:T(1024)}, u32[]{:S(2)}) copy-start(f32[2048]{0:T(1024)} %param.13) | copy-start | bytes 24580
  222.1 181.9 %reduce-scatter.8.cloned.1.call-start = ((), (), s32[]{:S(2)}) async-start(), calls=%async_computation.7 | async-start | bytes 4128768 | tf_op jit(solution)/shard_map/reduce_scatter | solution.py:43
  330.2 2.0 copy-start
  332.2 71.8 %copy-start.3 = (f32[64,1792]{1,0:T(8,128)S(1)}, f32[64,1792]{1,0:T(8,128)}, u32[]{:S(2)}) copy-start(f32[64,1792]{1,0:T(8,128)} %reduce-scatter.6.cloned.1.call-done) | copy-start | bytes 1376260
  332.2 71.8 %copy-start.6 = (f32[1792]{0:T(1024)S(1)}, f32[1792]{0:T(1024)}, u32[]{:S(2)}) copy-start(f32[1792]{0:T(1024)} %param.15) | copy-start | bytes 21508
  358.9 72.8 %all-gather.7.cloned.1.call-start = ((), (), s32[]{:S(2)}) async-start(), calls=%async_computation.8 | async-start | bytes 2064384 | tf_op jit(solution)/shard_map/all_gather | solution.py:45
  405.8 105.5 %all-reduce.6.cloned.1.call-start = ((), (), s32[]{:S(2)}) async-start(), calls=%async_computation.9 | async-start | bytes 4194304 | tf_op jit(solution)/shard_map/psum | solution.py:52
  448.2 128.4 %all-reduce.8.cloned.1.call-start = ((), (), s32[]{:S(2)}) async-start(), calls=%async_computation.10 | async-start | bytes 4194304 | tf_op jit(solution)/shard_map/psum | solution.py:52
  454.8 57.3 %copy-start.2 = (bf16[512,1792]{1,0:T(8,128)(2,1)S(1)}, bf16[512,1792]{1,0:T(8,128)(2,1)}, u32[]{:S(2)}) copy-start(bf16[512,1792]{1,0:T(8,128)(2,1)} %all-gather.7.cloned.1.call-done) | copy-start | bytes 5505028
  576.6 5.0 copy-start.1
  576.6 5.0 copy-start.4
Sparse Core Ops, SparseCore 0:
  9.6 45.2 all-gather.8
  77.9 78.4 reduce-scatter.3
  158.7 17.3 reduce-scatter.5
  178.2 26.9 all-gather.4
  222.2 103.0 all-reduce.3
  359.0 44.9 reduce-scatter.7
  406.2 25.3 all-gather.6
  448.3 62.8 all-reduce.5
  513.6 62.9 all-reduce.7
